TPU v7x, 256 devices: a whole 4x4x8 slice. The times are simulated.
256 devices in a mesh: row: 32 (over z, y_hi, core), off: 8 (over x, y_lo).
Axes of the slice: x: 4, y: 4 (y_hi: 2, y_lo: 2; y = y_hi * 2 + y_lo), z: 8, core: 2. Of those that a mesh axis runs over, the one named last changes fastest.
Arguments:
- vectors: float32 [32768, 128], P(('row', 'off')), may hold values from -6 to 6
- blocks: float32 [32, 8, 48, 128, 128], P('row', 'off'), may hold values from -0.0546875 to 0.0546875
- lists: int32 [32, 8, 2, 48], P('row', 'off'), may hold values from 0 to 7, as said below
Outputs:
- filtered: float32 [32768, 128], P(('row', 'off'))
Inputs may be any that keep to these rules, and one draw needn't show every extreme that they name: `lists`: within each tile the 48 listed blocks are distinct positions of its 8 x 8 grid of blocks.
All inputs are finite; a program needn't handle non-finite values.
Results may differ from a plain program's by a relative error of at most 0.00011.
Values sent between devices are 32-bit elements; how exact they have to be, the bound alone decides.
A program may use at most 64 MiB of HBM per device.

v0:
```python
import jax
import jax.numpy as jnp
from jax import lax
from jax.sharding import PartitionSpec as P

DEGREE = 4
first_scale = 0.4
later_scale = 0.8


def passed_along(block, axis, distance):
    devices = range(lax.axis_size(axis))
    route = [((i - distance) % len(devices), i) for i in devices]
    return lax.ppermute(block, axis, route)


def per_device(vectors, blocks, lists):
    n_offsets = lax.axis_size("off")
    offset_index = lax.axis_index("off")
    piece_rows = vectors.shape[0]
    tile_rows = piece_rows * n_offsets
    width = vectors.shape[1]
    block_size = blocks.shape[-1]
    per_side = tile_rows // block_size
    stored = blocks[0, 0]
    row_list = lists[0, 0, 0]
    col_list = lists[0, 0, 1]
    positions = jnp.arange(per_side, dtype=jnp.int32)
    row_onehot = (row_list[:, None] == positions[None, :]).astype(jnp.float32)
    col_onehot = (col_list[:, None] == positions[None, :]).astype(jnp.float32)
    bit_count = (n_offsets - 1).bit_length()

    def pull(field):
        for bit_number in range(bit_count):
            moved = passed_along(field, "row", -(1 << bit_number))
            field = jnp.where(offset_index // (1 << bit_number) % 2 == 1, moved, field)
        return field

    def push(field):
        for bit_number in range(bit_count):
            moved = passed_along(field, "row", 1 << bit_number)
            field = jnp.where(offset_index // (1 << bit_number) % 2 == 1, moved, field)
        return field

    def apply_tiles(gathered):
        own = gathered.reshape(per_side, block_size, width)
        transposed = jnp.einsum(
            "kab,kav->kbv", stored, own[row_list], precision=lax.Precision.HIGHEST
        )
        back_terms = jnp.einsum(
            "kt,kbv->tbv", col_onehot, transposed, precision=lax.Precision.HIGHEST
        )
        returned = push(back_terms.reshape(tile_rows, width))
        far_field = pull(gathered).reshape(per_side, block_size, width)
        direct = jnp.einsum(
            "kab,kbv->kav", stored, far_field[col_list], precision=lax.Precision.HIGHEST
        )
        ahead = jnp.einsum("kt,kav->tav", row_onehot, direct, precision=lax.Precision.HIGHEST)
        return ahead.reshape(tile_rows, width) + returned

    def spread(piece):
        return lax.all_gather(piece, "off", axis=0, tiled=True)

    def fold(terms):
        return lax.psum_scatter(terms, "off", scatter_dimension=0, tiled=True)

    previous = vectors
    current = first_scale * fold(apply_tiles(spread(vectors)))
    for degree in range(1, DEGREE):
        following = later_scale * fold(apply_tiles(spread(current))) - previous
        previous, current = (current, following)
    return current


def solution(mesh):
    in_specs = (
        P(("row", "off"), None),
        P("row", "off", None, None, None),
        P("row", "off", None, None),
    )
    out_specs = P(("row", "off"), None)
    return jax.shard_map(
        per_device, mesh=mesh, in_specs=in_specs, out_specs=out_specs, check_vma=False
    )
```

profile of v0, /device:TPU:32, one launch (start us, length us, event | category | flops | bytes accessed | tf_op | source)
XLA Modules:
  0.0 610.8 jit_solution(9065694514423480050)
XLA Ops:
  6.5 31.6 %all_gather.12 = f32[1024,128]{1,0:T(8,128)} all-gather(f32[128,128]{1,0:T(8,128)} %param.3), channel_id=1, replica_groups=mesh['row'=32,'off'=8] {'off'}, dimensions={0}, use_global_device_ids=true | all-gather | bytes 589824 | tf_op jit(solution)/shard_map/all_gather | solution.py:62
  38.9 3.5 gather_fusion.1
  42.4 7.9 %fusion.28 = f32[48,128,128]{2,1,0:T(8,128)} fusion(f32[48,128,128]{2,1,0:T(8,128)} %gather_fusion.1, f32[1,1,48,128,128]{4,3,2,1,0:T(8,128)S(1)} %copy-done), kind=kOutput, calls=%fused_computation.36 | convolution fusion | flops 1207959552 | bytes 9437184 | tf_op jit(solution)/shard_map/kab,kav->kbv/dot_general | solution.py:47
  50.2 3.6 copy.13
  53.8 3.0 fusion.12
  58.3 1.9 broadcast_select_fusion.7
  60.2 2.8 collective-permute-start.1
  62.9 6.2 %collective-permute-done.3 = f32[1024,128]{1,0:T(8,128)} collective-permute-done((f32[1024,128]{1,0:T(8,128)}, f32[1024,128]{1,0:T(8,128)}, u32[]{:S(2)}, u32[]{:S(2)}) %collective-permute-start.3) | collective-permute-done | bytes 524320 | tf_op jit(solution)/shard_map/ppermute | solution.py:14
  71.1 13.5 %collective-permute-start.4 = (f32[1024,128]{1,0:T(8,128)}, f32[1024,128]{1,0:T(8,128)}, u32[]{:S(2)}, u32[]{:S(2)}) collective-permute-start(f32[1024,128]{1,0:T(8,128)} %broadcast_select_fusion.6), channel_id=1, source_target_pairs={{240,0},{248,8},{0,16},{8,24},{16,32},{24,40},{32,48},{40,56},{48,... | collective-permute-start | bytes 1572872 | tf_op jit(solution)/shard_map/ppermute | solution.py:14
  84.5 1.9 broadcast_select_fusion.15
  86.6 10.5 %collective-permute-done.4 = f32[1024,128]{1,0:T(8,128)} collective-permute-done((f32[1024,128]{1,0:T(8,128)}, f32[1024,128]{1,0:T(8,128)}, u32[]{:S(2)}, u32[]{:S(2)}) %collective-permute-start.4) | collective-permute-done | bytes 524320 | tf_op jit(solution)/shard_map/ppermute | solution.py:14
  99.0 2.1 collective-permute-start.5
  103.1 3.5 gather_fusion
  106.5 7.9 %fusion.30 = f32[48,128,128]{2,1,0:T(8,128)} fusion(f32[48,128,128]{2,1,0:T(8,128)} %gather_fusion, f32[1,1,48,128,128]{4,3,2,1,0:T(8,128)S(1)} %copy-done), kind=kOutput, calls=%fused_computation.38 | convolution fusion | flops 1207959552 | bytes 9437184 | tf_op jit(solution)/shard_map/kab,kbv->kav/dot_general | solution.py:55
  114.4 3.6 copy.12
  118.0 3.0 fusion.14
  121.1 2.0 bitcast_add_fusion.3
  123.2 40.0 %reduce-scatter.5.cloned.1.call-done = f32[128,128]{1,0:T(8,128)} async-done(((f32[1024,128]{1,0:T(8,128)}), f32[128,128]{1,0:T(8,128)}) %reduce-scatter.5.cloned.1.call-update) | async-done | bytes 65552 | tf_op jit(solution)/shard_map/reduce_scatter | solution.py:65
  164.0 31.1 %all_gather.13 = f32[1024,128]{1,0:T(8,128)} all-gather(f32[128,128]{1,0:T(8,128)S(1)} %broadcast_multiply_fusion), channel_id=1, replica_groups=mesh['row'=32,'off'=8] {'off'}, dimensions={0}, use_global_device_ids=true | all-gather | bytes 589824 | tf_op jit(solution)/shard_map/all_gather | solution.py:62
  195.1 3.5 gather_fusion.3
  198.6 7.9 %fusion.24 = f32[48,128,128]{2,1,0:T(8,128)} fusion(f32[48,128,128]{2,1,0:T(8,128)} %gather_fusion.3, f32[1,1,48,128,128]{4,3,2,1,0:T(8,128)S(1)} %copy-done), kind=kOutput, calls=%fused_computation.32 | convolution fusion | flops 1207959552 | bytes 9437184 | tf_op jit(solution)/shard_map/kab,kav->kbv/dot_general | solution.py:47
  206.5 3.5 copy.15
  210.0 3.0 fusion.8
  214.8 2.8 collective-permute-start.7
  217.6 6.7 %collective-permute-done.9 = f32[1024,128]{1,0:T(8,128)S(1)} collective-permute-done((f32[1024,128]{1,0:T(8,128)S(1)}, f32[1024,128]{1,0:T(8,128)S(1)}, u32[]{:S(2)}, u32[]{:S(2)}) %collective-permute-start.9) | collective-permute-done | bytes 524320 | tf_op jit(solution)/shard_map/ppermute | solution.py:14
  224.4 12.9 %collective-permute-start.10 = (f32[1024,128]{1,0:T(8,128)S(1)}, f32[1024,128]{1,0:T(8,128)S(1)}, u32[]{:S(2)}, u32[]{:S(2)}) collective-permute-start(f32[1024,128]{1,0:T(8,128)S(1)} %broadcast_select_fusion.4), channel_id=1, source_target_pairs={{240,0},{248,8},{0,16},{8,24},{16,32},{24,40},{32,48},{40,56},{48,... | collective-permute-start | bytes 1572872 | tf_op jit(solution)/shard_map/ppermute | solution.py:14
  237.7 11.9 %collective-permute-done.10 = f32[1024,128]{1,0:T(8,128)S(1)} collective-permute-done((f32[1024,128]{1,0:T(8,128)S(1)}, f32[1024,128]{1,0:T(8,128)S(1)}, u32[]{:S(2)}, u32[]{:S(2)}) %collective-permute-start.10) | collective-permute-done | bytes 524320 | tf_op jit(solution)/shard_map/ppermute | solution.py:14
  253.0 3.4 gather_fusion.2
  256.4 7.9 %fusion.26 = f32[48,128,128]{2,1,0:T(8,128)} fusion(f32[48,128,128]{2,1,0:T(8,128)} %gather_fusion.2, f32[1,1,48,128,128]{4,3,2,1,0:T(8,128)S(1)} %copy-done), kind=kOutput, calls=%fused_computation.34 | convolution fusion | flops 1207959552 | bytes 9437184 | tf_op jit(solution)/shard_map/kab,kbv->kav/dot_general | solution.py:55
  264.3 3.6 copy.14
  267.9 3.0 fusion.10
  271.0 2.0 bitcast_add_fusion.2
  273.1 36.3 %reduce-scatter.7.cloned.1.call-done = f32[128,128]{1,0:T(8,128)} async-done(((f32[1024,128]{1,0:T(8,128)}), f32[128,128]{1,0:T(8,128)}) %reduce-scatter.7.cloned.1.call-update) | async-done | bytes 65552 | tf_op jit(solution)/shard_map/reduce_scatter | solution.py:65
  310.2 31.1 %all_gather.14 = f32[1024,128]{1,0:T(8,128)} all-gather(f32[128,128]{1,0:T(8,128)S(1)} %multiply_subtract_fusion.2), channel_id=1, replica_groups=mesh['row'=32,'off'=8] {'off'}, dimensions={0}, use_global_device_ids=true | all-gather | bytes 589824 | tf_op jit(solution)/shard_map/all_gather | solution.py:62
  341.5 3.5 gather_fusion.5
  345.0 7.9 %fusion.20 = f32[48,128,128]{2,1,0:T(8,128)} fusion(f32[48,128,128]{2,1,0:T(8,128)} %gather_fusion.5, f32[1,1,48,128,128]{4,3,2,1,0:T(8,128)S(1)} %copy-done), kind=kOutput, calls=%fused_computation.28 | convolution fusion | flops 1207959552 | bytes 9437184 | tf_op jit(solution)/shard_map/kab,kav->kbv/dot_general | solution.py:47
  352.8 3.5 copy.17
  356.4 3.0 fusion.4
  361.2 2.5 collective-permute-start.13
  363.6 7.0 %collective-permute-done.15 = f32[1024,128]{1,0:T(8,128)S(1)} collective-permute-done((f32[1024,128]{1,0:T(8,128)S(1)}, f32[1024,128]{1,0:T(8,128)S(1)}, u32[]{:S(2)}, u32[]{:S(2)}) %collective-permute-start.15) | collective-permute-done | bytes 524320 | tf_op jit(solution)/shard_map/ppermute | solution.py:14
  370.8 12.9 %collective-permute-start.16 = (f32[1024,128]{1,0:T(8,128)S(1)}, f32[1024,128]{1,0:T(8,128)S(1)}, u32[]{:S(2)}, u32[]{:S(2)}) collective-permute-start(f32[1024,128]{1,0:T(8,128)S(1)} %broadcast_select_fusion.2), channel_id=1, source_target_pairs={{240,0},{248,8},{0,16},{8,24},{16,32},{24,40},{32,48},{40,56},{48,... | collective-permute-start | bytes 1572872 | tf_op jit(solution)/shard_map/ppermute | solution.py:14
  384.2 11.9 %collective-permute-done.16 = f32[1024,128]{1,0:T(8,128)S(1)} collective-permute-done((f32[1024,128]{1,0:T(8,128)S(1)}, f32[1024,128]{1,0:T(8,128)S(1)}, u32[]{:S(2)}, u32[]{:S(2)}) %collective-permute-start.16) | collective-permute-done | bytes 524320 | tf_op jit(solution)/shard_map/ppermute | solution.py:14
  396.9 2.0 collective-permute-start.17
  399.8 3.4 gather_fusion.4
  403.2 7.9 %fusion.22 = f32[48,128,128]{2,1,0:T(8,128)} fusion(f32[48,128,128]{2,1,0:T(8,128)} %gather_fusion.4, f32[1,1,48,128,128]{4,3,2,1,0:T(8,128)S(1)} %copy-done), kind=kOutput, calls=%fused_computation.30 | convolution fusion | flops 1207959552 | bytes 9437184 | tf_op jit(solution)/shard_map/kab,kbv->kav/dot_general | solution.py:55
  411.1 3.6 copy.16
  414.6 3.0 fusion.6
  417.8 2.0 bitcast_add_fusion.1
  419.8 36.2 %reduce-scatter.9.cloned.1.call-done = f32[128,128]{1,0:T(8,128)} async-done(((f32[1024,128]{1,0:T(8,128)}), f32[128,128]{1,0:T(8,128)}) %reduce-scatter.9.cloned.1.call-update) | async-done | bytes 65552 | tf_op jit(solution)/shard_map/reduce_scatter | solution.py:65
  456.9 31.3 %all_gather.15 = f32[1024,128]{1,0:T(8,128)} all-gather(f32[128,128]{1,0:T(8,128)S(1)} %multiply_subtract_fusion.1), channel_id=1, replica_groups=mesh['row'=32,'off'=8] {'off'}, dimensions={0}, use_global_device_ids=true | all-gather | bytes 589824 | tf_op jit(solution)/shard_map/all_gather | solution.py:62
  488.2 3.5 gather_fusion.7
  491.7 7.9 %fusion.16 = f32[48,128,128]{2,1,0:T(8,128)} fusion(f32[48,128,128]{2,1,0:T(8,128)} %gather_fusion.7, f32[1,1,48,128,128]{4,3,2,1,0:T(8,128)S(1)} %copy-done), kind=kOutput, calls=%fused_computation.24 | convolution fusion | flops 1207959552 | bytes 9437184 | tf_op jit(solution)/shard_map/kab,kav->kbv/dot_general | solution.py:47
  499.6 3.6 copy.19
  503.1 3.0 fusion
  507.9 2.5 collective-permute-start.19
  510.5 7.0 %collective-permute-done.21 = f32[1024,128]{1,0:T(8,128)S(1)} collective-permute-done((f32[1024,128]{1,0:T(8,128)S(1)}, f32[1024,128]{1,0:T(8,128)S(1)}, u32[]{:S(2)}, u32[]{:S(2)}) %collective-permute-start.21) | collective-permute-done | bytes 524320 | tf_op jit(solution)/shard_map/ppermute | solution.py:14
  517.5 12.6 %collective-permute-start.22 = (f32[1024,128]{1,0:T(8,128)S(1)}, f32[1024,128]{1,0:T(8,128)S(1)}, u32[]{:S(2)}, u32[]{:S(2)}) collective-permute-start(f32[1024,128]{1,0:T(8,128)S(1)} %broadcast_select_fusion), channel_id=1, source_target_pairs={{240,0},{248,8},{0,16},{8,24},{16,32},{24,40},{32,48},{40,56},{48,... | collective-permute-start | bytes 1572872 | tf_op jit(solution)/shard_map/ppermute | solution.py:14
  530.7 11.8 %collective-permute-done.22 = f32[1024,128]{1,0:T(8,128)S(1)} collective-permute-done((f32[1024,128]{1,0:T(8,128)S(1)}, f32[1024,128]{1,0:T(8,128)S(1)}, u32[]{:S(2)}, u32[]{:S(2)}) %collective-permute-start.22) | collective-permute-done | bytes 524320 | tf_op jit(solution)/shard_map/ppermute | solution.py:14
  545.8 3.4 gather_fusion.6
  549.2 7.9 %fusion.18 = f32[48,128,128]{2,1,0:T(8,128)} fusion(f32[48,128,128]{2,1,0:T(8,128)} %gather_fusion.6, f32[1,1,48,128,128]{4,3,2,1,0:T(8,128)S(1)} %copy-done), kind=kOutput, calls=%fused_computation.26 | convolution fusion | flops 1207959552 | bytes 9437184 | tf_op jit(solution)/shard_map/kab,kbv->kav/dot_general | solution.py:55
  557.1 3.6 copy.18
  560.7 3.0 fusion.2
  563.8 2.0 bitcast_add_fusion
  565.9 36.5 %reduce-scatter.11.cloned.1.call-done = f32[128,128]{1,0:T(8,128)} async-done(((f32[1024,128]{1,0:T(8,128)}), f32[128,128]{1,0:T(8,128)}) %reduce-scatter.11.cloned.1.call-update) | async-done | bytes 65552 | tf_op jit(solution)/shard_map/reduce_scatter | solution.py:65
  (80 shorter events, 28.2 us)
Async XLA Ops:
  6.5 35.8 %copy-start = (f32[1,1,48,128,128]{4,3,2,1,0:T(8,128)S(1)}, f32[1,1,48,128,128]{4,3,2,1,0:T(8,128)}, u32[]{:S(2)}) copy-start(f32[1,1,48,128,128]{4,3,2,1,0:T(8,128)} %param.4) | copy-start | bytes 9437188
  6.5 156.6 %reduce-scatter.5.cloned.1.call-start = ((), (), s32[]{:S(2)}) async-start(), calls=%async_computation.4 | async-start | bytes 589824 | tf_op jit(solution)/shard_map/reduce_scatter | solution.py:65
  38.1 20.1 %collective-permute-start = (f32[1024,128]{1,0:T(8,128)}, f32[1024,128]{1,0:T(8,128)}, u32[]{:S(2)}, u32[]{:S(2)}) collective-permute-start(f32[1024,128]{1,0:T(8,128)} %all_gather.12), channel_id=1, source_target_pairs={{8,0},{16,8},{24,16},{32,24},{40,32},{48,40},{56,48},{64,56},{72,6... | collective-permute-start | bytes 1572872 | tf_op jit(solution)/shard_map/ppermute | solution.py:14
  50.2 3.6 copy-start.3
  57.7 11.4 %collective-permute-start.3 = (f32[1024,128]{1,0:T(8,128)}, f32[1024,128]{1,0:T(8,128)}, u32[]{:S(2)}, u32[]{:S(2)}) collective-permute-start(f32[1024,128]{1,0:T(8,128)} %bitcast.14), channel_id=1, source_target_pairs={{248,0},{0,8},{8,16},{16,24},{24,32},{32,40},{40,48},{48,56},{56,6... | collective-permute-start | bytes 1572872 | tf_op jit(solution)/shard_map/ppermute | solution.py:14
  60.2 24.3 %collective-permute-start.1 = (f32[1024,128]{1,0:T(8,128)}, f32[1024,128]{1,0:T(8,128)}, u32[]{:S(2)}, u32[]{:S(2)}) collective-permute-start(f32[1024,128]{1,0:T(8,128)} %broadcast_select_fusion.7), channel_id=1, source_target_pairs={{16,0},{24,8},{32,16},{40,24},{48,32},{56,40},{64,48},{72,56},{80,... | collective-permute-start | bytes 1572872 | tf_op jit(solution)/shard_map/ppermute | solution.py:14
  71.1 26.0 %collective-permute-start.4 = (f32[1024,128]{1,0:T(8,128)}, f32[1024,128]{1,0:T(8,128)}, u32[]{:S(2)}, u32[]{:S(2)}) collective-permute-start(f32[1024,128]{1,0:T(8,128)} %broadcast_select_fusion.6), channel_id=1, source_target_pairs={{240,0},{248,8},{0,16},{8,24},{16,32},{24,40},{32,48},{40,56},{48,... | collective-permute-start | bytes 1572872 | tf_op jit(solution)/shard_map/ppermute | solution.py:14
  86.4 14.7 %collective-permute-start.2 = (f32[1024,128]{1,0:T(8,128)}, f32[1024,128]{1,0:T(8,128)}, u32[]{:S(2)}, u32[]{:S(2)}) collective-permute-start(f32[1024,128]{1,0:T(8,128)} %broadcast_select_fusion.15), channel_id=1, source_target_pairs={{32,0},{40,8},{48,16},{56,24},{64,32},{72,40},{80,48},{88,56},{96,... | collective-permute-start | bytes 1572872 | tf_op jit(solution)/shard_map/ppermute | solution.py:14
  99.0 22.1 %collective-permute-start.5 = (f32[1024,128]{1,0:T(8,128)}, f32[1024,128]{1,0:T(8,128)}, u32[]{:S(2)}, u32[]{:S(2)}) collective-permute-start(f32[1024,128]{1,0:T(8,128)} %broadcast_select_fusion.14), channel_id=1, source_target_pairs={{224,0},{232,8},{240,16},{248,24},{0,32},{8,40},{16,48},{24,56},{3... | collective-permute-start | bytes 1572872 | tf_op jit(solution)/shard_map/ppermute | solution.py:14
  123.1 186.2 %reduce-scatter.7.cloned.1.call-start = ((), (), s32[]{:S(2)}) async-start(), calls=%async_computation.5 | async-start | bytes 589824 | tf_op jit(solution)/shard_map/reduce_scatter | solution.py:65
  195.1 18.6 %collective-permute-start.6 = (f32[1024,128]{1,0:T(8,128)}, f32[1024,128]{1,0:T(8,128)}, u32[]{:S(2)}, u32[]{:S(2)}) collective-permute-start(f32[1024,128]{1,0:T(8,128)} %all_gather.13), channel_id=1, source_target_pairs={{8,0},{16,8},{24,16},{32,24},{40,32},{48,40},{56,48},{64,56},{72,6... | collective-permute-start | bytes 1572872 | tf_op jit(solution)/shard_map/ppermute | solution.py:14
  213.1 11.2 %collective-permute-start.9 = (f32[1024,128]{1,0:T(8,128)S(1)}, f32[1024,128]{1,0:T(8,128)S(1)}, u32[]{:S(2)}, u32[]{:S(2)}) collective-permute-start(f32[1024,128]{1,0:T(8,128)S(1)} %bitcast.102), channel_id=1, source_target_pairs={{248,0},{0,8},{8,16},{16,24},{24,32},{32,40},{40,48},{48,56},{56,6... | collective-permute-start | bytes 1572872 | tf_op jit(solution)/shard_map/ppermute | solution.py:14
  214.8 22.5 %collective-permute-start.7 = (f32[1024,128]{1,0:T(8,128)S(1)}, f32[1024,128]{1,0:T(8,128)S(1)}, u32[]{:S(2)}, u32[]{:S(2)}) collective-permute-start(f32[1024,128]{1,0:T(8,128)S(1)} %broadcast_select_fusion.5), channel_id=1, source_target_pairs={{16,0},{24,8},{32,16},{40,24},{48,32},{56,40},{64,48},{72,56},{80,... | collective-permute-start | bytes 1572872 | tf_op jit(solution)/shard_map/ppermute | solution.py:14
  224.4 25.3 %collective-permute-start.10 = (f32[1024,128]{1,0:T(8,128)S(1)}, f32[1024,128]{1,0:T(8,128)S(1)}, u32[]{:S(2)}, u32[]{:S(2)}) collective-permute-start(f32[1024,128]{1,0:T(8,128)S(1)} %broadcast_select_fusion.4), channel_id=1, source_target_pairs={{240,0},{248,8},{0,16},{8,24},{16,32},{24,40},{32,48},{40,56},{48,... | collective-permute-start | bytes 1572872 | tf_op jit(solution)/shard_map/ppermute | solution.py:14
  237.3 14.8 %collective-permute-start.8 = (f32[1024,128]{1,0:T(8,128)S(1)}, f32[1024,128]{1,0:T(8,128)S(1)}, u32[]{:S(2)}, u32[]{:S(2)}) collective-permute-start(f32[1024,128]{1,0:T(8,128)S(1)} %broadcast_select_fusion.13), channel_id=1, source_target_pairs={{32,0},{40,8},{48,16},{56,24},{64,32},{72,40},{80,48},{88,56},{96,... | collective-permute-start | bytes 1572872 | tf_op jit(solution)/shard_map/ppermute | solution.py:14
  250.5 20.6 %collective-permute-start.11 = (f32[1024,128]{1,0:T(8,128)}, f32[1024,128]{1,0:T(8,128)}, u32[]{:S(2)}, u32[]{:S(2)}) collective-permute-start(f32[1024,128]{1,0:T(8,128)} %broadcast_select_fusion.12), channel_id=1, source_target_pairs={{224,0},{232,8},{240,16},{248,24},{0,32},{8,40},{16,48},{24,56},{3... | collective-permute-start | bytes 1572872 | tf_op jit(solution)/shard_map/ppermute | solution.py:14
  267.9 41.5 %copy-start.1 = (f32[128,128]{1,0:T(8,128)S(1)}, f32[128,128]{1,0:T(8,128)}, u32[]{:S(2)}) copy-start(f32[128,128]{1,0:T(8,128)} %param.3) | copy-start | bytes 196612
  273.0 183.0 %reduce-scatter.9.cloned.1.call-start = ((), (), s32[]{:S(2)}) async-start(), calls=%async_computation.6 | async-start | bytes 589824 | tf_op jit(solution)/shard_map/reduce_scatter | solution.py:65
  341.3 18.8 %collective-permute-start.12 = (f32[1024,128]{1,0:T(8,128)}, f32[1024,128]{1,0:T(8,128)}, u32[]{:S(2)}, u32[]{:S(2)}) collective-permute-start(f32[1024,128]{1,0:T(8,128)} %all_gather.14), channel_id=1, source_target_pairs={{8,0},{16,8},{24,16},{32,24},{40,32},{48,40},{56,48},{64,56},{72,6... | collective-permute-start | bytes 1572872 | tf_op jit(solution)/shard_map/ppermute | solution.py:14
  359.5 11.2 %collective-permute-start.15 = (f32[1024,128]{1,0:T(8,128)S(1)}, f32[1024,128]{1,0:T(8,128)S(1)}, u32[]{:S(2)}, u32[]{:S(2)}) collective-permute-start(f32[1024,128]{1,0:T(8,128)S(1)} %bitcast.103), channel_id=1, source_target_pairs={{248,0},{0,8},{8,16},{16,24},{24,32},{32,40},{40,48},{48,56},{56,6... | collective-permute-start | bytes 1572872 | tf_op jit(solution)/shard_map/ppermute | solution.py:14
  361.2 22.5 %collective-permute-start.13 = (f32[1024,128]{1,0:T(8,128)S(1)}, f32[1024,128]{1,0:T(8,128)S(1)}, u32[]{:S(2)}, u32[]{:S(2)}) collective-permute-start(f32[1024,128]{1,0:T(8,128)S(1)} %broadcast_select_fusion.3), channel_id=1, source_target_pairs={{16,0},{24,8},{32,16},{40,24},{48,32},{56,40},{64,48},{72,56},{80,... | collective-permute-start | bytes 1572872 | tf_op jit(solution)/shard_map/ppermute | solution.py:14
  370.8 25.3 %collective-permute-start.16 = (f32[1024,128]{1,0:T(8,128)S(1)}, f32[1024,128]{1,0:T(8,128)S(1)}, u32[]{:S(2)}, u32[]{:S(2)}) collective-permute-start(f32[1024,128]{1,0:T(8,128)S(1)} %broadcast_select_fusion.2), channel_id=1, source_target_pairs={{240,0},{248,8},{0,16},{8,24},{16,32},{24,40},{32,48},{40,56},{48,... | collective-permute-start | bytes 1572872 | tf_op jit(solution)/shard_map/ppermute | solution.py:14
  383.7 15.1 %collective-permute-start.14 = (f32[1024,128]{1,0:T(8,128)S(1)}, f32[1024,128]{1,0:T(8,128)S(1)}, u32[]{:S(2)}, u32[]{:S(2)}) collective-permute-start(f32[1024,128]{1,0:T(8,128)S(1)} %broadcast_select_fusion.11), channel_id=1, source_target_pairs={{32,0},{40,8},{48,16},{56,24},{64,32},{72,40},{80,48},{88,56},{96,... | collective-permute-start | bytes 1572872 | tf_op jit(solution)/shard_map/ppermute | solution.py:14
  396.9 20.9 %collective-permute-start.17 = (f32[1024,128]{1,0:T(8,128)}, f32[1024,128]{1,0:T(8,128)}, u32[]{:S(2)}, u32[]{:S(2)}) collective-permute-start(f32[1024,128]{1,0:T(8,128)} %broadcast_select_fusion.10), channel_id=1, source_target_pairs={{224,0},{232,8},{240,16},{248,24},{0,32},{8,40},{16,48},{24,56},{3... | collective-permute-start | bytes 1572872 | tf_op jit(solution)/shard_map/ppermute | solution.py:14
  414.6 41.4 %copy-start.2 = (f32[128,128]{1,0:T(8,128)S(1)}, f32[128,128]{1,0:T(8,128)}, u32[]{:S(2)}) copy-start(f32[128,128]{1,0:T(8,128)} %reduce-scatter.5.cloned.1.call-done) | copy-start | bytes 196612
  419.8 182.5 %reduce-scatter.11.cloned.1.call-start = ((), (), s32[]{:S(2)}) async-start(), calls=%async_computation.7 | async-start | bytes 589824 | tf_op jit(solution)/shard_map/reduce_scatter | solution.py:65
  488.2 18.6 %collective-permute-start.18 = (f32[1024,128]{1,0:T(8,128)}, f32[1024,128]{1,0:T(8,128)}, u32[]{:S(2)}, u32[]{:S(2)}) collective-permute-start(f32[1024,128]{1,0:T(8,128)} %all_gather.15), channel_id=1, source_target_pairs={{8,0},{16,8},{24,16},{32,24},{40,32},{48,40},{56,48},{64,56},{72,6... | collective-permute-start | bytes 1572872 | tf_op jit(solution)/shard_map/ppermute | solution.py:14
  506.3 11.2 %collective-permute-start.21 = (f32[1024,128]{1,0:T(8,128)S(1)}, f32[1024,128]{1,0:T(8,128)S(1)}, u32[]{:S(2)}, u32[]{:S(2)}) collective-permute-start(f32[1024,128]{1,0:T(8,128)S(1)} %bitcast.101), channel_id=1, source_target_pairs={{248,0},{0,8},{8,16},{16,24},{24,32},{32,40},{40,48},{48,56},{56,6... | collective-permute-start | bytes 1572872 | tf_op jit(solution)/shard_map/ppermute | solution.py:14
  507.9 22.2 %collective-permute-start.19 = (f32[1024,128]{1,0:T(8,128)S(1)}, f32[1024,128]{1,0:T(8,128)S(1)}, u32[]{:S(2)}, u32[]{:S(2)}) collective-permute-start(f32[1024,128]{1,0:T(8,128)S(1)} %broadcast_select_fusion.1), channel_id=1, source_target_pairs={{16,0},{24,8},{32,16},{40,24},{48,32},{56,40},{64,48},{72,56},{80,... | collective-permute-start | bytes 1572872 | tf_op jit(solution)/shard_map/ppermute | solution.py:14
  517.5 25.0 %collective-permute-start.22 = (f32[1024,128]{1,0:T(8,128)S(1)}, f32[1024,128]{1,0:T(8,128)S(1)}, u32[]{:S(2)}, u32[]{:S(2)}) collective-permute-start(f32[1024,128]{1,0:T(8,128)S(1)} %broadcast_select_fusion), channel_id=1, source_target_pairs={{240,0},{248,8},{0,16},{8,24},{16,32},{24,40},{32,48},{40,56},{48,... | collective-permute-start | bytes 1572872 | tf_op jit(solution)/shard_map/ppermute | solution.py:14
  530.2 14.7 %collective-permute-start.20 = (f32[1024,128]{1,0:T(8,128)S(1)}, f32[1024,128]{1,0:T(8,128)S(1)}, u32[]{:S(2)}, u32[]{:S(2)}) collective-permute-start(f32[1024,128]{1,0:T(8,128)S(1)} %broadcast_select_fusion.9), channel_id=1, source_target_pairs={{32,0},{40,8},{48,16},{56,24},{64,32},{72,40},{80,48},{88,56},{96,... | collective-permute-start | bytes 1572872 | tf_op jit(solution)/shard_map/ppermute | solution.py:14
  543.4 20.4 %collective-permute-start.23 = (f32[1024,128]{1,0:T(8,128)}, f32[1024,128]{1,0:T(8,128)}, u32[]{:S(2)}, u32[]{:S(2)}) collective-permute-start(f32[1024,128]{1,0:T(8,128)} %broadcast_select_fusion.8), channel_id=1, source_target_pairs={{224,0},{232,8},{240,16},{248,24},{0,32},{8,40},{16,48},{24,56},{3... | collective-permute-start | bytes 1572872 | tf_op jit(solution)/shard_map/ppermute | solution.py:14
Sparse Core Ops, SparseCore 0:
  123.3 39.8 reduce-scatter.4
  273.2 36.1 reduce-scatter.6
  419.9 36.1 reduce-scatter.8
  566.0 36.2 reduce-scatter.10
where the time goes:
time: 619 us; the launch traced here: 611 us
  waiting for transfers between devices  222 us (36%)
  blocking collectives  125 us (20%)
  matrix products  87.2 us (14%)
  starting transfers between devices  73.7 us (12%)
  local copies, waits for them, and re-layouts  57.9 us (9%)
  other arithmetic  31.1 us (5%)
  between operations  13.7 us (2%)
    reduce_scatter x4, waiting for transfers between devices, fold(): return lax.psum_scatter(terms, 'off', scatter_dimension=0, tiled=True)  149 us
    all_gather x4, blocking collectives, spread(): return lax.all_gather(piece, 'off', axis=0, tiled=True)  125 us
    ppermute x24, starting transfers between devices, passed_along(): return lax.ppermute(block, axis, route)  73.5 us
    ppermute x24, waiting for transfers between devices, passed_along(): return lax.ppermute(block, axis, route)  73.1 us
    dot_general x4, matrix products, apply_tiles(): jnp.einsum('kab,kav->kbv', stored, own[row_list], precision=lax.Precision...  31.5 us
    dot_general x4, matrix products, apply_tiles(): jnp.einsum('kab,kbv->kav', stored, far_field[col_list], precision=lax.Pre...  31.5 us
    dot_general x4, local copies, waits for them, and re-layouts, apply_tiles(): jnp.einsum('kab,kbv->kav', stored, far_field[col_list], precision=lax.Pre...  14.3 us
    dot_general x4, local copies, waits for them, and re-layouts, apply_tiles(): jnp.einsum('kab,kav->kbv', stored, own[row_list], precision=lax.Precision...  14.3 us
  transfers between devices with their start and end apart: 28, of which 12 were waited for; matrix products, arithmetic and copies ran while one was open for 27% of the time, Pallas kernels for 0%

commit v1 on v0

--- a/solution.py
+++ b/solution.py
@@ -6,6 +6,13 @@
 DEGREE = 4
 first_scale = 0.4
 later_scale = 0.8
+
+
+def all_by_exchange(x, name, dim):
+    size = lax.axis_size(name)
+    blocks = jnp.stack([x for _ in range(size)])
+    blocks = lax.all_to_all(blocks, name, split_axis=0, concat_axis=0)
+    return jnp.concatenate(blocks, axis=dim)
 
 
 def passed_along(block, axis, distance):
@@ -59,7 +66,7 @@
         return ahead.reshape(tile_rows, width) + returned
 
     def spread(piece):
-        return lax.all_gather(piece, "off", axis=0, tiled=True)
+        return all_by_exchange(piece, "off", 0)
 
     def fold(terms):
         return lax.psum_scatter(terms, "off", scatter_dimension=0, tiled=True)

time: 619 us -> 547 us (0.88)
  blocking collectives: 125 us -> 34.3 us
  waiting for transfers between devices: 222 us -> 233 us
    all_gather x4 -> x0, blocking collectives: 125 us -> none  [spread(): return lax.all_gather(piece, 'off', axis=0, tiled=True)]
    all_to_all x0 -> x3, blocking collectives: none -> 34.3 us  [all_by_exchange(): blocks = lax.all_to_all(blocks, name, split_axis=0, concat_axis=0)]
    all_to_all x0 -> x1, waiting for transfers between devices: none -> 7.99 us  [all_by_exchange(): blocks = lax.all_to_all(blocks, name, split_axis=0, concat_axis=0)]
  transfers between devices with their start and end apart: 28 -> 29, of which waited for: 12 -> 13; matrix products, arithmetic and copies ran while one was open for 27% -> 31% of each run, Pallas kernels for 0% -> 0%
where the time goes in v1:
time: 547 us; the launch traced here: 538 us
  waiting for transfers between devices  233 us (43%)
  matrix products  87.5 us (16%)
  starting transfers between devices  78.6 us (14%)
  local copies, waits for them, and re-layouts  60.7 us (11%)
  blocking collectives  34.3 us (6%)
  other arithmetic  30.9 us (6%)
  between operations  13.8 us (3%)
    reduce_scatter x4, waiting for transfers between devices, fold(): return lax.psum_scatter(terms, 'off', scatter_dimension=0, tiled=True)  151 us
    ppermute x24, waiting for transfers between devices, passed_along(): return lax.ppermute(block, axis, route)  73.5 us
    ppermute x24, starting transfers between devices, passed_along(): return lax.ppermute(block, axis, route)  73.1 us
    all_to_all x3, blocking collectives, all_by_exchange(): blocks = lax.all_to_all(blocks, name, split_axis=0, concat_axis=0)  34.3 us
    dot_general x4, matrix products, apply_tiles(): jnp.einsum('kab,kbv->kav', stored, far_field[col_list], precision=lax.Pre...  31.7 us
    dot_general x4, matrix products, apply_tiles(): jnp.einsum('kab,kav->kbv', stored, own[row_list], precision=lax.Precision...  31.5 us
    dot_general x4, local copies, waits for them, and re-layouts, apply_tiles(): jnp.einsum('kab,kav->kbv', stored, own[row_list], precision=lax.Precision...  14.4 us
    dot_general x4, local copies, waits for them, and re-layouts, apply_tiles(): jnp.einsum('kab,kbv->kav', stored, far_field[col_list], precision=lax.Pre...  14.3 us
  transfers between devices with their start and end apart: 29, of which 13 were waited for; matrix products, arithmetic and copies ran while one was open for 31% of the time, Pallas kernels for 0%

profile of v1, /device:TPU:32, one launch (start us, length us, event | category | flops | bytes accessed | tf_op | source)
XLA Modules:
  0.0 538.2 jit_solution(873811269976412089)
XLA Ops:
  8.4 5.3 all-to-all-start
  15.3 8.0 %all-to-all-done = f32[8,128,128]{2,1,0:T(8,128)} async-done(((f32[8,128,128]{2,1,0:T(8,128)}), f32[8,128,128]{2,1,0:T(8,128)}, u32[]{:S(2)}, u32[]{:S(2)}) %all-to-all-start) | async-done | bytes 524320 | tf_op jit(solution)/shard_map/all_to_all | solution.py:14
  24.1 3.5 gather_fusion.1
  27.6 7.9 %fusion.28 = f32[48,128,128]{2,1,0:T(8,128)} fusion(f32[48,128,128]{2,1,0:T(8,128)} %gather_fusion.1, f32[1,1,48,128,128]{4,3,2,1,0:T(8,128)S(1)} %copy-done), kind=kOutput, calls=%fused_computation.36 | convolution fusion | flops 1207959552 | bytes 9437184 | tf_op jit(solution)/shard_map/kab,kav->kbv/dot_general | solution.py:54
  35.5 3.6 copy.13
  39.1 3.0 fusion.12
  43.0 1.9 broadcast_select_fusion.7
  44.9 2.1 collective-permute-start.1
  47.0 7.4 %collective-permute-done.3 = f32[1024,128]{1,0:T(8,128)} collective-permute-done((f32[1024,128]{1,0:T(8,128)}, f32[1024,128]{1,0:T(8,128)}, u32[]{:S(2)}, u32[]{:S(2)}) %collective-permute-start.3) | collective-permute-done | bytes 524320 | tf_op jit(solution)/shard_map/ppermute | solution.py:21
  56.3 12.3 %collective-permute-start.4 = (f32[1024,128]{1,0:T(8,128)}, f32[1024,128]{1,0:T(8,128)}, u32[]{:S(2)}, u32[]{:S(2)}) collective-permute-start(f32[1024,128]{1,0:T(8,128)} %broadcast_select_fusion.6), channel_id=1, source_target_pairs={{240,0},{248,8},{0,16},{8,24},{16,32},{24,40},{32,48},{40,56},{48,... | collective-permute-start | bytes 1572872 | tf_op jit(solution)/shard_map/ppermute | solution.py:21
  68.6 1.9 broadcast_select_fusion.15
  70.7 10.6 %collective-permute-done.4 = f32[1024,128]{1,0:T(8,128)} collective-permute-done((f32[1024,128]{1,0:T(8,128)}, f32[1024,128]{1,0:T(8,128)}, u32[]{:S(2)}, u32[]{:S(2)}) %collective-permute-start.4) | collective-permute-done | bytes 524320 | tf_op jit(solution)/shard_map/ppermute | solution.py:21
  83.1 2.1 collective-permute-start.5
  87.1 3.4 gather_fusion
  90.6 7.9 %fusion.30 = f32[48,128,128]{2,1,0:T(8,128)} fusion(f32[48,128,128]{2,1,0:T(8,128)} %gather_fusion, f32[1,1,48,128,128]{4,3,2,1,0:T(8,128)S(1)} %copy-done), kind=kOutput, calls=%fused_computation.38 | convolution fusion | flops 1207959552 | bytes 9437184 | tf_op jit(solution)/shard_map/kab,kbv->kav/dot_general | solution.py:62
  98.5 3.6 copy.12
  102.1 3.0 fusion.14
  105.2 2.0 bitcast_add_fusion.3
  107.2 38.9 %reduce-scatter.5.cloned.1.call-done = f32[128,128]{1,0:T(8,128)} async-done(((f32[1024,128]{1,0:T(8,128)}), f32[128,128]{1,0:T(8,128)}) %reduce-scatter.5.cloned.1.call-update) | async-done | bytes 65552 | tf_op jit(solution)/shard_map/reduce_scatter | solution.py:72
  147.0 11.4 %all_to_all.20 = f32[8,128,128]{2,1,0:T(8,128)} all-to-all(f32[8,128,128]{2,1,0:T(8,128)S(1)} %stack.9), channel_id=1, replica_groups=mesh['row'=32,'off'=8] {'off'}, dimensions={0} | all-to-all | bytes 1048576 | tf_op jit(solution)/shard_map/all_to_all | solution.py:14
  158.4 3.5 gather_fusion.3
  162.0 7.9 %fusion.24 = f32[48,128,128]{2,1,0:T(8,128)} fusion(f32[48,128,128]{2,1,0:T(8,128)} %gather_fusion.3, f32[1,1,48,128,128]{4,3,2,1,0:T(8,128)S(1)} %copy-done), kind=kOutput, calls=%fused_computation.32 | convolution fusion | flops 1207959552 | bytes 9437184 | tf_op jit(solution)/shard_map/kab,kav->kbv/dot_general | solution.py:54
  169.8 3.6 copy.15
  173.4 3.0 fusion.8
  178.2 3.2 collective-permute-start.7
  181.4 6.4 %collective-permute-done.9 = f32[1024,128]{1,0:T(8,128)S(1)} collective-permute-done((f32[1024,128]{1,0:T(8,128)S(1)}, f32[1024,128]{1,0:T(8,128)S(1)}, u32[]{:S(2)}, u32[]{:S(2)}) %collective-permute-start.9) | collective-permute-done | bytes 524320 | tf_op jit(solution)/shard_map/ppermute | solution.py:21
  187.8 13.0 %collective-permute-start.10 = (f32[1024,128]{1,0:T(8,128)S(1)}, f32[1024,128]{1,0:T(8,128)S(1)}, u32[]{:S(2)}, u32[]{:S(2)}) collective-permute-start(f32[1024,128]{1,0:T(8,128)S(1)} %broadcast_select_fusion.4), channel_id=1, source_target_pairs={{240,0},{248,8},{0,16},{8,24},{16,32},{24,40},{32,48},{40,56},{48,... | collective-permute-start | bytes 1572872 | tf_op jit(solution)/shard_map/ppermute | solution.py:21
  201.5 11.7 %collective-permute-done.10 = f32[1024,128]{1,0:T(8,128)S(1)} collective-permute-done((f32[1024,128]{1,0:T(8,128)S(1)}, f32[1024,128]{1,0:T(8,128)S(1)}, u32[]{:S(2)}, u32[]{:S(2)}) %collective-permute-start.10) | collective-permute-done | bytes 524320 | tf_op jit(solution)/shard_map/ppermute | solution.py:21
  216.5 3.4 gather_fusion.2
  219.9 7.9 %fusion.26 = f32[48,128,128]{2,1,0:T(8,128)} fusion(f32[48,128,128]{2,1,0:T(8,128)} %gather_fusion.2, f32[1,1,48,128,128]{4,3,2,1,0:T(8,128)S(1)} %copy-done), kind=kOutput, calls=%fused_computation.34 | convolution fusion | flops 1207959552 | bytes 9437184 | tf_op jit(solution)/shard_map/kab,kbv->kav/dot_general | solution.py:62
  227.8 3.6 copy.14
  231.4 3.0 fusion.10
  234.6 2.0 bitcast_add_fusion.2
  236.6 37.2 %reduce-scatter.7.cloned.1.call-done = f32[128,128]{1,0:T(8,128)} async-done(((f32[1024,128]{1,0:T(8,128)}), f32[128,128]{1,0:T(8,128)}) %reduce-scatter.7.cloned.1.call-update) | async-done | bytes 65552 | tf_op jit(solution)/shard_map/reduce_scatter | solution.py:72
  274.7 11.4 %all_to_all.21 = f32[8,128,128]{2,1,0:T(8,128)} all-to-all(f32[8,128,128]{2,1,0:T(8,128)S(1)} %stack.10), channel_id=1, replica_groups=mesh['row'=32,'off'=8] {'off'}, dimensions={0} | all-to-all | bytes 1048576 | tf_op jit(solution)/shard_map/all_to_all | solution.py:14
  286.3 3.5 gather_fusion.5
  289.8 7.9 %fusion.20 = f32[48,128,128]{2,1,0:T(8,128)} fusion(f32[48,128,128]{2,1,0:T(8,128)} %gather_fusion.5, f32[1,1,48,128,128]{4,3,2,1,0:T(8,128)S(1)} %copy-done), kind=kOutput, calls=%fused_computation.28 | convolution fusion | flops 1207959552 | bytes 9437184 | tf_op jit(solution)/shard_map/kab,kav->kbv/dot_general | solution.py:54
  297.7 3.6 copy.17
  301.3 3.0 fusion.4
  306.1 2.6 collective-permute-start.13
  308.7 6.9 %collective-permute-done.15 = f32[1024,128]{1,0:T(8,128)S(1)} collective-permute-done((f32[1024,128]{1,0:T(8,128)S(1)}, f32[1024,128]{1,0:T(8,128)S(1)}, u32[]{:S(2)}, u32[]{:S(2)}) %collective-permute-start.15) | collective-permute-done | bytes 524320 | tf_op jit(solution)/shard_map/ppermute | solution.py:21
  315.7 13.1 %collective-permute-start.16 = (f32[1024,128]{1,0:T(8,128)S(1)}, f32[1024,128]{1,0:T(8,128)S(1)}, u32[]{:S(2)}, u32[]{:S(2)}) collective-permute-start(f32[1024,128]{1,0:T(8,128)S(1)} %broadcast_select_fusion.2), channel_id=1, source_target_pairs={{240,0},{248,8},{0,16},{8,24},{16,32},{24,40},{32,48},{40,56},{48,... | collective-permute-start | bytes 1572872 | tf_op jit(solution)/shard_map/ppermute | solution.py:21
  329.2 11.9 %collective-permute-done.16 = f32[1024,128]{1,0:T(8,128)S(1)} collective-permute-done((f32[1024,128]{1,0:T(8,128)S(1)}, f32[1024,128]{1,0:T(8,128)S(1)}, u32[]{:S(2)}, u32[]{:S(2)}) %collective-permute-start.16) | collective-permute-done | bytes 524320 | tf_op jit(solution)/shard_map/ppermute | solution.py:21
  344.4 3.4 gather_fusion.4
  347.8 7.9 %fusion.22 = f32[48,128,128]{2,1,0:T(8,128)} fusion(f32[48,128,128]{2,1,0:T(8,128)} %gather_fusion.4, f32[1,1,48,128,128]{4,3,2,1,0:T(8,128)S(1)} %copy-done), kind=kOutput, calls=%fused_computation.30 | convolution fusion | flops 1207959552 | bytes 9437184 | tf_op jit(solution)/shard_map/kab,kbv->kav/dot_general | solution.py:62
  355.8 3.6 copy.16
  359.4 3.0 fusion.6
  362.5 2.0 bitcast_add_fusion.1
  364.5 37.5 %reduce-scatter.9.cloned.1.call-done = f32[128,128]{1,0:T(8,128)} async-done(((f32[1024,128]{1,0:T(8,128)}), f32[128,128]{1,0:T(8,128)}) %reduce-scatter.9.cloned.1.call-update) | async-done | bytes 65552 | tf_op jit(solution)/shard_map/reduce_scatter | solution.py:72
  403.0 11.4 %all_to_all.22 = f32[8,128,128]{2,1,0:T(8,128)} all-to-all(f32[8,128,128]{2,1,0:T(8,128)S(1)} %stack.11), channel_id=1, replica_groups=mesh['row'=32,'off'=8] {'off'}, dimensions={0} | all-to-all | bytes 1048576 | tf_op jit(solution)/shard_map/all_to_all | solution.py:14
  414.4 3.5 gather_fusion.7
  417.9 7.9 %fusion.16 = f32[48,128,128]{2,1,0:T(8,128)} fusion(f32[48,128,128]{2,1,0:T(8,128)} %gather_fusion.7, f32[1,1,48,128,128]{4,3,2,1,0:T(8,128)S(1)} %copy-done), kind=kOutput, calls=%fused_computation.24 | convolution fusion | flops 1207959552 | bytes 9437184 | tf_op jit(solution)/shard_map/kab,kav->kbv/dot_general | solution.py:54
  425.8 3.6 copy.19
  429.4 3.0 fusion
  434.2 2.8 collective-permute-start.19
  437.0 6.7 %collective-permute-done.21 = f32[1024,128]{1,0:T(8,128)S(1)} collective-permute-done((f32[1024,128]{1,0:T(8,128)S(1)}, f32[1024,128]{1,0:T(8,128)S(1)}, u32[]{:S(2)}, u32[]{:S(2)}) %collective-permute-start.21) | collective-permute-done | bytes 524320 | tf_op jit(solution)/shard_map/ppermute | solution.py:21
  443.8 13.0 %collective-permute-start.22 = (f32[1024,128]{1,0:T(8,128)S(1)}, f32[1024,128]{1,0:T(8,128)S(1)}, u32[]{:S(2)}, u32[]{:S(2)}) collective-permute-start(f32[1024,128]{1,0:T(8,128)S(1)} %broadcast_select_fusion), channel_id=1, source_target_pairs={{240,0},{248,8},{0,16},{8,24},{16,32},{24,40},{32,48},{40,56},{48,... | collective-permute-start | bytes 1572872 | tf_op jit(solution)/shard_map/ppermute | solution.py:21
  457.3 11.8 %collective-permute-done.22 = f32[1024,128]{1,0:T(8,128)S(1)} collective-permute-done((f32[1024,128]{1,0:T(8,128)S(1)}, f32[1024,128]{1,0:T(8,128)S(1)}, u32[]{:S(2)}, u32[]{:S(2)}) %collective-permute-start.22) | collective-permute-done | bytes 524320 | tf_op jit(solution)/shard_map/ppermute | solution.py:21
  472.4 3.4 gather_fusion.6
  475.8 7.9 %fusion.18 = f32[48,128,128]{2,1,0:T(8,128)} fusion(f32[48,128,128]{2,1,0:T(8,128)} %gather_fusion.6, f32[1,1,48,128,128]{4,3,2,1,0:T(8,128)S(1)} %copy-done), kind=kOutput, calls=%fused_computation.26 | convolution fusion | flops 1207959552 | bytes 9437184 | tf_op jit(solution)/shard_map/kab,kbv->kav/dot_general | solution.py:62
  483.7 3.6 copy.18
  487.3 3.0 fusion.2
  490.4 2.0 bitcast_add_fusion
  492.4 37.3 %reduce-scatter.11.cloned.1.call-done = f32[128,128]{1,0:T(8,128)} async-done(((f32[1024,128]{1,0:T(8,128)}), f32[128,128]{1,0:T(8,128)}) %reduce-scatter.11.cloned.1.call-update) | async-done | bytes 65552 | tf_op jit(solution)/shard_map/reduce_scatter | solution.py:72
  (83 shorter events, 32.8 us)
Async XLA Ops:
  6.5 21.1 %copy-start = (f32[1,1,48,128,128]{4,3,2,1,0:T(8,128)S(1)}, f32[1,1,48,128,128]{4,3,2,1,0:T(8,128)}, u32[]{:S(2)}) copy-start(f32[1,1,48,128,128]{4,3,2,1,0:T(8,128)} %param.4) | copy-start | bytes 9437188
  8.4 14.9 %all-to-all-start = ((f32[8,128,128]{2,1,0:T(8,128)}), f32[8,128,128]{2,1,0:T(8,128)}, u32[]{:S(2)}, u32[]{:S(2)}) async-start(f32[8,128,128]{2,1,0:T(8,128)} %stack.8), calls=%async_computation | async-start | bytes 1048576 | tf_op jit(solution)/shard_map/all_to_all | solution.py:14
  13.7 132.5 %reduce-scatter.5.cloned.1.call-start = ((), (), s32[]{:S(2)}) async-start(), calls=%async_computation.8 | async-start | bytes 589824 | tf_op jit(solution)/shard_map/reduce_scatter | solution.py:72
  23.3 19.8 %collective-permute-start = (f32[1024,128]{1,0:T(8,128)}, f32[1024,128]{1,0:T(8,128)}, u32[]{:S(2)}, u32[]{:S(2)}) collective-permute-start(f32[1024,128]{1,0:T(8,128)} %bitcast.2), channel_id=1, source_target_pairs={{8,0},{16,8},{24,16},{32,24},{40,32},{48,40},{56,48},{64,56},{72,6... | collective-permute-start | bytes 1572872 | tf_op jit(solution)/shard_map/ppermute | solution.py:21
  43.0 11.4 %collective-permute-start.3 = (f32[1024,128]{1,0:T(8,128)}, f32[1024,128]{1,0:T(8,128)}, u32[]{:S(2)}, u32[]{:S(2)}) collective-permute-start(f32[1024,128]{1,0:T(8,128)} %bitcast.14), channel_id=1, source_target_pairs={{248,0},{0,8},{8,16},{16,24},{24,32},{32,40},{40,48},{48,56},{56,6... | collective-permute-start | bytes 1572872 | tf_op jit(solution)/shard_map/ppermute | solution.py:21
  44.9 23.7 %collective-permute-start.1 = (f32[1024,128]{1,0:T(8,128)}, f32[1024,128]{1,0:T(8,128)}, u32[]{:S(2)}, u32[]{:S(2)}) collective-permute-start(f32[1024,128]{1,0:T(8,128)} %broadcast_select_fusion.7), channel_id=1, source_target_pairs={{16,0},{24,8},{32,16},{40,24},{48,32},{56,40},{64,48},{72,56},{80,... | collective-permute-start | bytes 1572872 | tf_op jit(solution)/shard_map/ppermute | solution.py:21
  56.3 24.9 %collective-permute-start.4 = (f32[1024,128]{1,0:T(8,128)}, f32[1024,128]{1,0:T(8,128)}, u32[]{:S(2)}, u32[]{:S(2)}) collective-permute-start(f32[1024,128]{1,0:T(8,128)} %broadcast_select_fusion.6), channel_id=1, source_target_pairs={{240,0},{248,8},{0,16},{8,24},{16,32},{24,40},{32,48},{40,56},{48,... | collective-permute-start | bytes 1572872 | tf_op jit(solution)/shard_map/ppermute | solution.py:21
  70.5 14.7 %collective-permute-start.2 = (f32[1024,128]{1,0:T(8,128)}, f32[1024,128]{1,0:T(8,128)}, u32[]{:S(2)}, u32[]{:S(2)}) collective-permute-start(f32[1024,128]{1,0:T(8,128)} %broadcast_select_fusion.15), channel_id=1, source_target_pairs={{32,0},{40,8},{48,16},{56,24},{64,32},{72,40},{80,48},{88,56},{96,... | collective-permute-start | bytes 1572872 | tf_op jit(solution)/shard_map/ppermute | solution.py:21
  83.1 22.1 %collective-permute-start.5 = (f32[1024,128]{1,0:T(8,128)}, f32[1024,128]{1,0:T(8,128)}, u32[]{:S(2)}, u32[]{:S(2)}) collective-permute-start(f32[1024,128]{1,0:T(8,128)} %broadcast_select_fusion.14), channel_id=1, source_target_pairs={{224,0},{232,8},{240,16},{248,24},{0,32},{8,40},{16,48},{24,56},{3... | collective-permute-start | bytes 1572872 | tf_op jit(solution)/shard_map/ppermute | solution.py:21
  107.2 166.6 %reduce-scatter.7.cloned.1.call-start = ((), (), s32[]{:S(2)}) async-start(), calls=%async_computation.9 | async-start | bytes 589824 | tf_op jit(solution)/shard_map/reduce_scatter | solution.py:72
  158.4 18.7 %collective-permute-start.6 = (f32[1024,128]{1,0:T(8,128)}, f32[1024,128]{1,0:T(8,128)}, u32[]{:S(2)}, u32[]{:S(2)}) collective-permute-start(f32[1024,128]{1,0:T(8,128)} %bitcast.15), channel_id=1, source_target_pairs={{8,0},{16,8},{24,16},{32,24},{40,32},{48,40},{56,48},{64,56},{72,6... | collective-permute-start | bytes 1572872 | tf_op jit(solution)/shard_map/ppermute | solution.py:21
  176.6 11.2 %collective-permute-start.9 = (f32[1024,128]{1,0:T(8,128)S(1)}, f32[1024,128]{1,0:T(8,128)S(1)}, u32[]{:S(2)}, u32[]{:S(2)}) collective-permute-start(f32[1024,128]{1,0:T(8,128)S(1)} %bitcast.106), channel_id=1, source_target_pairs={{248,0},{0,8},{8,16},{16,24},{24,32},{32,40},{40,48},{48,56},{56,6... | collective-permute-start | bytes 1572872 | tf_op jit(solution)/shard_map/ppermute | solution.py:21
  178.2 22.6 %collective-permute-start.7 = (f32[1024,128]{1,0:T(8,128)S(1)}, f32[1024,128]{1,0:T(8,128)S(1)}, u32[]{:S(2)}, u32[]{:S(2)}) collective-permute-start(f32[1024,128]{1,0:T(8,128)S(1)} %broadcast_select_fusion.5), channel_id=1, source_target_pairs={{16,0},{24,8},{32,16},{40,24},{48,32},{56,40},{64,48},{72,56},{80,... | collective-permute-start | bytes 1572872 | tf_op jit(solution)/shard_map/ppermute | solution.py:21
  187.8 25.4 %collective-permute-start.10 = (f32[1024,128]{1,0:T(8,128)S(1)}, f32[1024,128]{1,0:T(8,128)S(1)}, u32[]{:S(2)}, u32[]{:S(2)}) collective-permute-start(f32[1024,128]{1,0:T(8,128)S(1)} %broadcast_select_fusion.4), channel_id=1, source_target_pairs={{240,0},{248,8},{0,16},{8,24},{16,32},{24,40},{32,48},{40,56},{48,... | collective-permute-start | bytes 1572872 | tf_op jit(solution)/shard_map/ppermute | solution.py:21
  200.9 14.7 %collective-permute-start.8 = (f32[1024,128]{1,0:T(8,128)S(1)}, f32[1024,128]{1,0:T(8,128)S(1)}, u32[]{:S(2)}, u32[]{:S(2)}) collective-permute-start(f32[1024,128]{1,0:T(8,128)S(1)} %broadcast_select_fusion.13), channel_id=1, source_target_pairs={{32,0},{40,8},{48,16},{56,24},{64,32},{72,40},{80,48},{88,56},{96,... | collective-permute-start | bytes 1572872 | tf_op jit(solution)/shard_map/ppermute | solution.py:21
  214.0 20.5 %collective-permute-start.11 = (f32[1024,128]{1,0:T(8,128)}, f32[1024,128]{1,0:T(8,128)}, u32[]{:S(2)}, u32[]{:S(2)}) collective-permute-start(f32[1024,128]{1,0:T(8,128)} %broadcast_select_fusion.12), channel_id=1, source_target_pairs={{224,0},{232,8},{240,16},{248,24},{0,32},{8,40},{16,48},{24,56},{3... | collective-permute-start | bytes 1572872 | tf_op jit(solution)/shard_map/ppermute | solution.py:21
  231.4 42.4 %copy-start.1 = (f32[128,128]{1,0:T(8,128)S(1)}, f32[128,128]{1,0:T(8,128)}, u32[]{:S(2)}) copy-start(f32[128,128]{1,0:T(8,128)} %param.3) | copy-start | bytes 196612
  236.5 165.5 %reduce-scatter.9.cloned.1.call-start = ((), (), s32[]{:S(2)}) async-start(), calls=%async_computation.10 | async-start | bytes 589824 | tf_op jit(solution)/shard_map/reduce_scatter | solution.py:72
  286.1 18.8 %collective-permute-start.12 = (f32[1024,128]{1,0:T(8,128)}, f32[1024,128]{1,0:T(8,128)}, u32[]{:S(2)}, u32[]{:S(2)}) collective-permute-start(f32[1024,128]{1,0:T(8,128)} %bitcast.21), channel_id=1, source_target_pairs={{8,0},{16,8},{24,16},{32,24},{40,32},{48,40},{56,48},{64,56},{72,6... | collective-permute-start | bytes 1572872 | tf_op jit(solution)/shard_map/ppermute | solution.py:21
  304.4 11.2 %collective-permute-start.15 = (f32[1024,128]{1,0:T(8,128)S(1)}, f32[1024,128]{1,0:T(8,128)S(1)}, u32[]{:S(2)}, u32[]{:S(2)}) collective-permute-start(f32[1024,128]{1,0:T(8,128)S(1)} %bitcast.107), channel_id=1, source_target_pairs={{248,0},{0,8},{8,16},{16,24},{24,32},{32,40},{40,48},{48,56},{56,6... | collective-permute-start | bytes 1572872 | tf_op jit(solution)/shard_map/ppermute | solution.py:21
  306.1 22.7 %collective-permute-start.13 = (f32[1024,128]{1,0:T(8,128)S(1)}, f32[1024,128]{1,0:T(8,128)S(1)}, u32[]{:S(2)}, u32[]{:S(2)}) collective-permute-start(f32[1024,128]{1,0:T(8,128)S(1)} %broadcast_select_fusion.3), channel_id=1, source_target_pairs={{16,0},{24,8},{32,16},{40,24},{48,32},{56,40},{64,48},{72,56},{80,... | collective-permute-start | bytes 1572872 | tf_op jit(solution)/shard_map/ppermute | solution.py:21
  315.7 25.4 %collective-permute-start.16 = (f32[1024,128]{1,0:T(8,128)S(1)}, f32[1024,128]{1,0:T(8,128)S(1)}, u32[]{:S(2)}, u32[]{:S(2)}) collective-permute-start(f32[1024,128]{1,0:T(8,128)S(1)} %broadcast_select_fusion.2), channel_id=1, source_target_pairs={{240,0},{248,8},{0,16},{8,24},{16,32},{24,40},{32,48},{40,56},{48,... | collective-permute-start | bytes 1572872 | tf_op jit(solution)/shard_map/ppermute | solution.py:21
  328.8 14.7 %collective-permute-start.14 = (f32[1024,128]{1,0:T(8,128)S(1)}, f32[1024,128]{1,0:T(8,128)S(1)}, u32[]{:S(2)}, u32[]{:S(2)}) collective-permute-start(f32[1024,128]{1,0:T(8,128)S(1)} %broadcast_select_fusion.11), channel_id=1, source_target_pairs={{32,0},{40,8},{48,16},{56,24},{64,32},{72,40},{80,48},{88,56},{96,... | collective-permute-start | bytes 1572872 | tf_op jit(solution)/shard_map/ppermute | solution.py:21
  341.9 20.6 %collective-permute-start.17 = (f32[1024,128]{1,0:T(8,128)}, f32[1024,128]{1,0:T(8,128)}, u32[]{:S(2)}, u32[]{:S(2)}) collective-permute-start(f32[1024,128]{1,0:T(8,128)} %broadcast_select_fusion.10), channel_id=1, source_target_pairs={{224,0},{232,8},{240,16},{248,24},{0,32},{8,40},{16,48},{24,56},{3... | collective-permute-start | bytes 1572872 | tf_op jit(solution)/shard_map/ppermute | solution.py:21
  359.3 42.7 %copy-start.2 = (f32[128,128]{1,0:T(8,128)S(1)}, f32[128,128]{1,0:T(8,128)}, u32[]{:S(2)}) copy-start(f32[128,128]{1,0:T(8,128)} %reduce-scatter.5.cloned.1.call-done) | copy-start | bytes 196612
  364.5 165.2 %reduce-scatter.11.cloned.1.call-start = ((), (), s32[]{:S(2)}) async-start(), calls=%async_computation.11 | async-start | bytes 589824 | tf_op jit(solution)/shard_map/reduce_scatter | solution.py:72
  414.4 18.7 %collective-permute-start.18 = (f32[1024,128]{1,0:T(8,128)}, f32[1024,128]{1,0:T(8,128)}, u32[]{:S(2)}, u32[]{:S(2)}) collective-permute-start(f32[1024,128]{1,0:T(8,128)} %bitcast.27), channel_id=1, source_target_pairs={{8,0},{16,8},{24,16},{32,24},{40,32},{48,40},{56,48},{64,56},{72,6... | collective-permute-start | bytes 1572872 | tf_op jit(solution)/shard_map/ppermute | solution.py:21
  432.5 11.2 %collective-permute-start.21 = (f32[1024,128]{1,0:T(8,128)S(1)}, f32[1024,128]{1,0:T(8,128)S(1)}, u32[]{:S(2)}, u32[]{:S(2)}) collective-permute-start(f32[1024,128]{1,0:T(8,128)S(1)} %bitcast.105), channel_id=1, source_target_pairs={{248,0},{0,8},{8,16},{16,24},{24,32},{32,40},{40,48},{48,56},{56,6... | collective-permute-start | bytes 1572872 | tf_op jit(solution)/shard_map/ppermute | solution.py:21
  434.2 22.6 %collective-permute-start.19 = (f32[1024,128]{1,0:T(8,128)S(1)}, f32[1024,128]{1,0:T(8,128)S(1)}, u32[]{:S(2)}, u32[]{:S(2)}) collective-permute-start(f32[1024,128]{1,0:T(8,128)S(1)} %broadcast_select_fusion.1), channel_id=1, source_target_pairs={{16,0},{24,8},{32,16},{40,24},{48,32},{56,40},{64,48},{72,56},{80,... | collective-permute-start | bytes 1572872 | tf_op jit(solution)/shard_map/ppermute | solution.py:21
  443.8 25.3 %collective-permute-start.22 = (f32[1024,128]{1,0:T(8,128)S(1)}, f32[1024,128]{1,0:T(8,128)S(1)}, u32[]{:S(2)}, u32[]{:S(2)}) collective-permute-start(f32[1024,128]{1,0:T(8,128)S(1)} %broadcast_select_fusion), channel_id=1, source_target_pairs={{240,0},{248,8},{0,16},{8,24},{16,32},{24,40},{32,48},{40,56},{48,... | collective-permute-start | bytes 1572872 | tf_op jit(solution)/shard_map/ppermute | solution.py:21
  456.8 14.7 %collective-permute-start.20 = (f32[1024,128]{1,0:T(8,128)S(1)}, f32[1024,128]{1,0:T(8,128)S(1)}, u32[]{:S(2)}, u32[]{:S(2)}) collective-permute-start(f32[1024,128]{1,0:T(8,128)S(1)} %broadcast_select_fusion.9), channel_id=1, source_target_pairs={{32,0},{40,8},{48,16},{56,24},{64,32},{72,40},{80,48},{88,56},{96,... | collective-permute-start | bytes 1572872 | tf_op jit(solution)/shard_map/ppermute | solution.py:21
  469.9 20.5 %collective-permute-start.23 = (f32[1024,128]{1,0:T(8,128)}, f32[1024,128]{1,0:T(8,128)}, u32[]{:S(2)}, u32[]{:S(2)}) collective-permute-start(f32[1024,128]{1,0:T(8,128)} %broadcast_select_fusion.8), channel_id=1, source_target_pairs={{224,0},{232,8},{240,16},{248,24},{0,32},{8,40},{16,48},{24,56},{3... | collective-permute-start | bytes 1572872 | tf_op jit(solution)/shard_map/ppermute | solution.py:21
Sparse Core Ops, SparseCore 0:
  107.3 38.7 reduce-scatter.4
  236.7 37.1 reduce-scatter.6
  364.6 37.4 reduce-scatter.8
  492.5 37.1 reduce-scatter.10
